TPU v7x, 128 devices: a whole 4x4x4 slice. The times are simulated.
128 devices in a mesh: walk: 16 (over y_hi, z, core), band: 8 (over y_lo, x).
Axes of the slice: x: 4, y: 4 (y_hi: 2, y_lo: 2; y = y_hi * 2 + y_lo), z: 4, core: 2. Of those that a mesh axis runs over, the one named last changes fastest.
Arguments:
- positions: float32 [2, 49152], P(None, 'walk'), may hold values from 0 to 1
- coefficients: bfloat16 [2, 18432, 1024], P(None, 'walk', 'band')
- lattice: int32 [2, 18432], replicated, may hold values from -76 to 76
- spin_labels: int32 [49152], P('walk'), may hold values from 0 to 1
- occupied: int32 [2, 48], replicated, may hold values from 0 to 1023
- features: bfloat16 [49152, 256], P('walk'), may hold values from -6 to 6
- orbital_head: bfloat16 [256, 192], replicated, may hold values from -0.029907227 to 0.029907227
Outputs:
- gradient: float32 [256, 192], replicated
All inputs are finite; a program needn't handle non-finite values.
Results may differ from a plain program's by a relative error of at most 0.0003.
Values may be sent and summed in bfloat16 or wider, within the bound.
No kernel may reach another device: no remote copies, remote signals or barrier semaphores. Data moves between devices by JAX's collectives and lax.ppermute only.
A program may use at most 128 MiB of HBM per device.

v0:
```python
import jax
import jax.numpy as jnp
from jax import lax
from jax.sharding import PartitionSpec as P

E = 96
TWO_PI = 6.283185307179586


def orbital_block(pos_x, pos_y, lat_x, lat_y, right_cos, right_sin):
    phase_angle = TWO_PI * (pos_x[:, None] * lat_x[None, :] + pos_y[:, None] * lat_y[None, :])
    cosine = jnp.cos(phase_angle)
    sine_part = jnp.sin(phase_angle)
    first = jnp.dot(
        cosine, right_cos, precision=lax.Precision.HIGHEST, preferred_element_type=jnp.float32
    )
    second = jnp.dot(
        sine_part, right_sin, precision=lax.Precision.HIGHEST, preferred_element_type=jnp.float32
    )
    return first + second


def spin_columns(orbitals, spin_labels):
    orbital_count = orbitals.shape[1] // 4
    spin_up = (spin_labels == 0)[:, None]
    real_pick = jnp.where(
        spin_up, orbitals[:, :orbital_count], orbitals[:, orbital_count : 2 * orbital_count]
    )
    imag_pick = jnp.where(
        spin_up,
        orbitals[:, 2 * orbital_count : 3 * orbital_count],
        orbitals[:, 3 * orbital_count :],
    )
    return jnp.concatenate([real_pick, imag_pick], axis=1)


def fit_from_target(target, spin_labels, features, orbital_head, walkers):
    half_width = target.shape[1]
    spin_up = (spin_labels == 0)[:, None]
    net_all = jnp.dot(features, orbital_head, preferred_element_type=jnp.float32)
    net_value = jnp.where(spin_up, net_all[:, :half_width], net_all[:, half_width:])
    scaled = (net_value - target) / walkers
    blank_rows = jnp.zeros_like(scaled)
    spread_rows = jnp.concatenate(
        [jnp.where(spin_up, scaled, blank_rows), jnp.where(spin_up, blank_rows, scaled)], axis=1
    )
    return lax.dot_general(
        features.astype(jnp.float32),
        spread_rows,
        (((0,), (0,)), ((), ())),
        precision=lax.Precision.HIGHEST,
        preferred_element_type=jnp.float32,
    )


def fit_gradient(orbitals, spin_labels, features, orbital_head, walkers):
    target = spin_columns(orbitals, spin_labels)
    return fit_from_target(target, spin_labels, features, orbital_head, walkers)


def local(positions, coefficients, lattice, spin_labels, occupied, features, orbital_head):
    walk_count = lax.axis_size("walk")
    band_count = lax.axis_size("band")
    band_index = lax.axis_index("band")
    occ_flat = occupied.reshape(-1)
    wave_count = lattice.shape[1]
    gathered = lax.all_gather(coefficients, "walk", axis=1, tiled=True)
    band_panel = lax.all_to_all(gathered, "band", split_axis=1, concat_axis=2, tiled=True)
    picked = jnp.take(band_panel, occ_flat, axis=2)
    local_lattice = lax.dynamic_slice_in_dim(
        lattice, band_index * (wave_count // band_count), wave_count // band_count, 1
    )
    right_cos = jnp.concatenate([picked[0], picked[1]], axis=1).astype(jnp.float32)
    right_sin = jnp.concatenate([-picked[1], picked[0]], axis=1).astype(jnp.float32)
    lat_x = local_lattice[0].astype(jnp.float32)
    lat_y = local_lattice[1].astype(jnp.float32)
    local_count = positions.shape[1]
    block_rows = min(384, local_count)
    block_count = local_count // block_rows
    pos_x = positions[0].reshape(block_count, block_rows)
    pos_y = positions[1].reshape(block_count, block_rows)
    partial_value = lax.map(
        lambda coords: orbital_block(coords[0], coords[1], lat_x, lat_y, right_cos, right_sin),
        (pos_x, pos_y),
    )
    partial_value = partial_value.reshape(local_count, right_cos.shape[1])
    walkers = float(walk_count * local_count // E)
    orbitals = lax.psum(partial_value, "band")
    gradient = fit_gradient(orbitals, spin_labels, features, orbital_head, walkers)
    return lax.psum(gradient, "walk")


def solution(mesh):
    return jax.shard_map(
        local,
        mesh=mesh,
        in_specs=(
            P(None, "walk"),
            P(None, "walk", "band"),
            P(),
            P("walk"),
            P(),
            P("walk", None),
            P(),
        ),
        out_specs=P(),
        check_vma=False,
    )
```

profile of v0, /device:TPU:0, one launch (start us, length us, event | category | flops | bytes accessed | tf_op | source)
XLA Modules:
  0.0 891.4 jit_solution(2126646476932792642)
XLA Ops:
  6.5 6.1 copy.31
  12.7 79.9 %all-gather.2.cloned.1.call-done = bf16[2,18432,128]{2,0,1:T(2,128)(2,1)} async-done(((bf16[2,1152,128]{2,0,1:T(2,128)(2,1)}), bf16[2,18432,128]{2,0,1:T(2,128)(2,1)}) %all-gather.2.cloned.1.call-update) | async-done | bytes 9437200 | tf_op jit(solution)/shard_map/all_gather | solution.py:67
  92.5 5.0 all-to-all-start
  97.9 0.9 fusion.32
  98.9 105.0 %all-to-all-done = bf16[2,18432,128]{2,0,1:T(2,128)(2,1)} async-done(((bf16[2,18432,128]{2,0,1:T(2,128)(2,1)}), bf16[2,18432,128]{2,0,1:T(2,128)(2,1)}, u32[]{:S(2)}, u32[]{:S(2)}) %all-to-all-start) | async-done | bytes 9437216 | tf_op jit(solution)/shard_map/all_to_all | solution.py:68
  203.9 10.1 %copy.32 = bf16[2,18432,128]{2,1,0:T(8,128)(2,1)} copy(bf16[2,18432,128]{2,0,1:T(2,128)(2,1)} %all-to-all-done) | data formatting | bytes 18874368 | tf_op jit(solution)/shard_map/all_to_all | solution.py:68
  214.0 12.9 %copy.33 = bf16[2,2304,8,128]{1,3,2,0:T(8,128)(2,1)} copy(bf16[2,2304,8,128]{3,1,2,0:T(8,128)(2,1)} %bitcast.33) | data formatting | bytes 18874368 | tf_op jit(solution)/shard_map/all_to_all | solution.py:68
  226.9 18.4 %copy.34 = bf16[2,2304,1024]{1,0,2:T(2,128)(2,1)} copy(bf16[2,2304,1024]{1,2,0:T(8,128)(2,1)} %bitcast.34) | data formatting | bytes 18874368 | tf_op jit(solution)/shard_map/all_to_all | solution.py:68
  245.3 6.1 gather_fusion
  251.4 0.8 fusion.31
  252.2 1.2 fusion.37
  253.6 1.5 maximum_convert_fusion.1
  255.0 3.0 copy.35
  258.0 1.9 copy.36
  259.9 364.3 %while.10 = (s32[]{:T(128)}, f32[8,384,192]{1,0,2:T(8,128)}, f32[8,384]{1,0:T(8,128)S(1)}, f32[2304]{0:T(1024)S(1)}, f32[8,384]{1,0:T(8,128)S(1)}, /*index=5*/f3...) while((s32[]{:T(128)}, f32[8,384,192]{1,0,2:T(8,128)}, ...), condition=%wide.region_1.2_spmd, body=%wide.region_0.1_spmd.sunk | while | flops 4084015104 | bytes 12730505 | solution.py:82
  282.6 18.3 %fusion.54 = f32[384,192]{0,1:T(8,128)S(1)} fusion(f32[2304,192]{1,0:T(8,128)} %get-tuple-element.200, f32[2304]{0:T(1024)S(1)} %get-tuple-element.198, f32[384]{0:T(512)S(1)} %get-tuple-element.171, f32[2304]{0:T(1024)S(1)} %get-tuple-element.196, f32[384]{0:T(512)S(1)} %get-tuple-element.172), kind=kOutput, calls=%fused_computation.1.clone.1 | convolution fusion | flops 2041970688 | bytes 2085888 | tf_op jit(solution)/shard_map/while/body/eval_jaxpr/dot_general | solution.py:17
  300.9 16.4 %fusion.55 = f32[1,384,192]{1,2,0:T(8,128)S(1)} fusion(f32[384,192]{0,1:T(8,128)S(1)} %fusion.54, f32[2304,192]{1,0:T(8,128)S(1)} %copy-done.2, f32[2304]{0:T(1024)S(1)} %get-tuple-element.198, f32[384]{0:T(512)S(1)} %get-tuple-element.171, f32[2304]{0:T(1024)S(1)} %get-tuple-element.196, f32[384]{0:T(512)S(1)} %get-tuple-element.172), kind=kOutput, calls=%fused_computation.17.clone.1 | convolution fusion | flops 2042044416 | bytes 2380800 | tf_op jit(solution)/shard_map/while/body/eval_jaxpr/dot_general | solution.py:14
  317.7 7.3 dynamic_update_slice.5
  325.0 18.3 %fusion.54 = f32[384,192]{0,1:T(8,128)S(1)} fusion(f32[2304,192]{1,0:T(8,128)} %get-tuple-element.200, f32[2304]{0:T(1024)S(1)} %get-tuple-element.198, f32[384]{0:T(512)S(1)} %get-tuple-element.171, f32[2304]{0:T(1024)S(1)} %get-tuple-element.196, f32[384]{0:T(512)S(1)} %get-tuple-element.172), kind=kOutput, calls=%fused_computation.1.clone.1 | convolution fusion | flops 2041970688 | bytes 2085888 | tf_op jit(solution)/shard_map/while/body/eval_jaxpr/dot_general | solution.py:17
  343.3 16.4 %fusion.55 = f32[1,384,192]{1,2,0:T(8,128)S(1)} fusion(f32[384,192]{0,1:T(8,128)S(1)} %fusion.54, f32[2304,192]{1,0:T(8,128)S(1)} %copy-done.2, f32[2304]{0:T(1024)S(1)} %get-tuple-element.198, f32[384]{0:T(512)S(1)} %get-tuple-element.171, f32[2304]{0:T(1024)S(1)} %get-tuple-element.196, f32[384]{0:T(512)S(1)} %get-tuple-element.172), kind=kOutput, calls=%fused_computation.17.clone.1 | convolution fusion | flops 2042044416 | bytes 2380800 | tf_op jit(solution)/shard_map/while/body/eval_jaxpr/dot_general | solution.py:14
  360.0 7.3 dynamic_update_slice.5
  367.4 18.3 %fusion.54 = f32[384,192]{0,1:T(8,128)S(1)} fusion(f32[2304,192]{1,0:T(8,128)} %get-tuple-element.200, f32[2304]{0:T(1024)S(1)} %get-tuple-element.198, f32[384]{0:T(512)S(1)} %get-tuple-element.171, f32[2304]{0:T(1024)S(1)} %get-tuple-element.196, f32[384]{0:T(512)S(1)} %get-tuple-element.172), kind=kOutput, calls=%fused_computation.1.clone.1 | convolution fusion | flops 2041970688 | bytes 2085888 | tf_op jit(solution)/shard_map/while/body/eval_jaxpr/dot_general | solution.py:17
  385.7 16.4 %fusion.55 = f32[1,384,192]{1,2,0:T(8,128)S(1)} fusion(f32[384,192]{0,1:T(8,128)S(1)} %fusion.54, f32[2304,192]{1,0:T(8,128)S(1)} %copy-done.2, f32[2304]{0:T(1024)S(1)} %get-tuple-element.198, f32[384]{0:T(512)S(1)} %get-tuple-element.171, f32[2304]{0:T(1024)S(1)} %get-tuple-element.196, f32[384]{0:T(512)S(1)} %get-tuple-element.172), kind=kOutput, calls=%fused_computation.17.clone.1 | convolution fusion | flops 2042044416 | bytes 2380800 | tf_op jit(solution)/shard_map/while/body/eval_jaxpr/dot_general | solution.py:14
  402.4 7.3 dynamic_update_slice.5
  409.7 18.3 %fusion.54 = f32[384,192]{0,1:T(8,128)S(1)} fusion(f32[2304,192]{1,0:T(8,128)} %get-tuple-element.200, f32[2304]{0:T(1024)S(1)} %get-tuple-element.198, f32[384]{0:T(512)S(1)} %get-tuple-element.171, f32[2304]{0:T(1024)S(1)} %get-tuple-element.196, f32[384]{0:T(512)S(1)} %get-tuple-element.172), kind=kOutput, calls=%fused_computation.1.clone.1 | convolution fusion | flops 2041970688 | bytes 2085888 | tf_op jit(solution)/shard_map/while/body/eval_jaxpr/dot_general | solution.py:17
  428.1 16.4 %fusion.55 = f32[1,384,192]{1,2,0:T(8,128)S(1)} fusion(f32[384,192]{0,1:T(8,128)S(1)} %fusion.54, f32[2304,192]{1,0:T(8,128)S(1)} %copy-done.2, f32[2304]{0:T(1024)S(1)} %get-tuple-element.198, f32[384]{0:T(512)S(1)} %get-tuple-element.171, f32[2304]{0:T(1024)S(1)} %get-tuple-element.196, f32[384]{0:T(512)S(1)} %get-tuple-element.172), kind=kOutput, calls=%fused_computation.17.clone.1 | convolution fusion | flops 2042044416 | bytes 2380800 | tf_op jit(solution)/shard_map/while/body/eval_jaxpr/dot_general | solution.py:14
  444.8 7.3 dynamic_update_slice.5
  452.1 18.3 %fusion.54 = f32[384,192]{0,1:T(8,128)S(1)} fusion(f32[2304,192]{1,0:T(8,128)} %get-tuple-element.200, f32[2304]{0:T(1024)S(1)} %get-tuple-element.198, f32[384]{0:T(512)S(1)} %get-tuple-element.171, f32[2304]{0:T(1024)S(1)} %get-tuple-element.196, f32[384]{0:T(512)S(1)} %get-tuple-element.172), kind=kOutput, calls=%fused_computation.1.clone.1 | convolution fusion | flops 2041970688 | bytes 2085888 | tf_op jit(solution)/shard_map/while/body/eval_jaxpr/dot_general | solution.py:17
  470.4 16.4 %fusion.55 = f32[1,384,192]{1,2,0:T(8,128)S(1)} fusion(f32[384,192]{0,1:T(8,128)S(1)} %fusion.54, f32[2304,192]{1,0:T(8,128)S(1)} %copy-done.2, f32[2304]{0:T(1024)S(1)} %get-tuple-element.198, f32[384]{0:T(512)S(1)} %get-tuple-element.171, f32[2304]{0:T(1024)S(1)} %get-tuple-element.196, f32[384]{0:T(512)S(1)} %get-tuple-element.172), kind=kOutput, calls=%fused_computation.17.clone.1 | convolution fusion | flops 2042044416 | bytes 2380800 | tf_op jit(solution)/shard_map/while/body/eval_jaxpr/dot_general | solution.py:14
  487.2 7.3 dynamic_update_slice.5
  494.5 18.3 %fusion.54 = f32[384,192]{0,1:T(8,128)S(1)} fusion(f32[2304,192]{1,0:T(8,128)} %get-tuple-element.200, f32[2304]{0:T(1024)S(1)} %get-tuple-element.198, f32[384]{0:T(512)S(1)} %get-tuple-element.171, f32[2304]{0:T(1024)S(1)} %get-tuple-element.196, f32[384]{0:T(512)S(1)} %get-tuple-element.172), kind=kOutput, calls=%fused_computation.1.clone.1 | convolution fusion | flops 2041970688 | bytes 2085888 | tf_op jit(solution)/shard_map/while/body/eval_jaxpr/dot_general | solution.py:17
  512.8 16.4 %fusion.55 = f32[1,384,192]{1,2,0:T(8,128)S(1)} fusion(f32[384,192]{0,1:T(8,128)S(1)} %fusion.54, f32[2304,192]{1,0:T(8,128)S(1)} %copy-done.2, f32[2304]{0:T(1024)S(1)} %get-tuple-element.198, f32[384]{0:T(512)S(1)} %get-tuple-element.171, f32[2304]{0:T(1024)S(1)} %get-tuple-element.196, f32[384]{0:T(512)S(1)} %get-tuple-element.172), kind=kOutput, calls=%fused_computation.17.clone.1 | convolution fusion | flops 2042044416 | bytes 2380800 | tf_op jit(solution)/shard_map/while/body/eval_jaxpr/dot_general | solution.py:14
  529.5 7.3 dynamic_update_slice.5
  536.9 18.3 %fusion.54 = f32[384,192]{0,1:T(8,128)S(1)} fusion(f32[2304,192]{1,0:T(8,128)} %get-tuple-element.200, f32[2304]{0:T(1024)S(1)} %get-tuple-element.198, f32[384]{0:T(512)S(1)} %get-tuple-element.171, f32[2304]{0:T(1024)S(1)} %get-tuple-element.196, f32[384]{0:T(512)S(1)} %get-tuple-element.172), kind=kOutput, calls=%fused_computation.1.clone.1 | convolution fusion | flops 2041970688 | bytes 2085888 | tf_op jit(solution)/shard_map/while/body/eval_jaxpr/dot_general | solution.py:17
  555.2 16.4 %fusion.55 = f32[1,384,192]{1,2,0:T(8,128)S(1)} fusion(f32[384,192]{0,1:T(8,128)S(1)} %fusion.54, f32[2304,192]{1,0:T(8,128)S(1)} %copy-done.2, f32[2304]{0:T(1024)S(1)} %get-tuple-element.198, f32[384]{0:T(512)S(1)} %get-tuple-element.171, f32[2304]{0:T(1024)S(1)} %get-tuple-element.196, f32[384]{0:T(512)S(1)} %get-tuple-element.172), kind=kOutput, calls=%fused_computation.17.clone.1 | convolution fusion | flops 2042044416 | bytes 2380800 | tf_op jit(solution)/shard_map/while/body/eval_jaxpr/dot_general | solution.py:14
  571.9 7.3 dynamic_update_slice.5
  579.2 18.3 %fusion.54 = f32[384,192]{0,1:T(8,128)S(1)} fusion(f32[2304,192]{1,0:T(8,128)} %get-tuple-element.200, f32[2304]{0:T(1024)S(1)} %get-tuple-element.198, f32[384]{0:T(512)S(1)} %get-tuple-element.171, f32[2304]{0:T(1024)S(1)} %get-tuple-element.196, f32[384]{0:T(512)S(1)} %get-tuple-element.172), kind=kOutput, calls=%fused_computation.1.clone.1 | convolution fusion | flops 2041970688 | bytes 2085888 | tf_op jit(solution)/shard_map/while/body/eval_jaxpr/dot_general | solution.py:17
  597.6 16.4 %fusion.55 = f32[1,384,192]{1,2,0:T(8,128)S(1)} fusion(f32[384,192]{0,1:T(8,128)S(1)} %fusion.54, f32[2304,192]{1,0:T(8,128)S(1)} %copy-done.2, f32[2304]{0:T(1024)S(1)} %get-tuple-element.198, f32[384]{0:T(512)S(1)} %get-tuple-element.171, f32[2304]{0:T(1024)S(1)} %get-tuple-element.196, f32[384]{0:T(512)S(1)} %get-tuple-element.172), kind=kOutput, calls=%fused_computation.17.clone.1 | convolution fusion | flops 2042044416 | bytes 2380800 | tf_op jit(solution)/shard_map/while/body/eval_jaxpr/dot_general | solution.py:14
  614.3 7.3 dynamic_update_slice.5
  624.2 3.5 copy.42
  627.8 0.6 copy-done.5
  628.6 2.1 fusion.38
  630.7 114.0 %all-reduce.3.cloned.1.call-done = f32[3072,192]{0,1:T(8,128)} async-done(((f32[3072,192]{0,1:T(8,128)}), f32[3072,192]{0,1:T(8,128)}) %all-reduce.3.cloned.1.call-update) | async-done | bytes 2359312 | tf_op jit(solution)/shard_map/psum | solution.py:88
  744.7 1.9 slice_select_fusion.2
  746.6 0.5 copy-done.1
  747.5 1.9 fusion.28
  749.4 133.6 %all-reduce.5.cloned.1.call-done = f32[256,192]{0,1:T(8,128)} async-done(((f32[256,192]{0,1:T(8,128)}), f32[256,192]{0,1:T(8,128)}) %all-reduce.5.cloned.1.call-update) | async-done | bytes 196624 | tf_op jit(solution)/shard_map/psum | solution.py:90
  883.0 1.6 copy.58
  (61 shorter events, 3.8 us)
Async XLA Ops:
  6.5 621.9 %copy-start = (bf16[3072,256]{1,0:T(8,128)(2,1)S(1)}, bf16[3072,256]{1,0:T(8,128)(2,1)}, u32[]{:S(2)}) copy-start(bf16[3072,256]{1,0:T(8,128)(2,1)} %param.14) | copy-start | bytes 4718596
  6.5 86.0 %all-gather.2.cloned.1.call-start = ((), (), s32[]{:S(2)}) async-start(), calls=%async_computation.1 | async-start | bytes 10027008 | tf_op jit(solution)/shard_map/all_gather | solution.py:67
  12.6 85.0 %copy-start.6 = (s32[2,48]{1,0:T(2,128)S(1)}, s32[2,48]{1,0:T(2,128)}, u32[]{:S(2)}) copy-start(s32[2,48]{1,0:T(2,128)} %param.13) | copy-start | bytes 1156
  12.6 85.2 %copy-start.4 = (f32[2,3072]{1,0:T(2,128)S(1)}, f32[2,3072]{1,0:T(2,128)}, u32[]{:S(2)}) copy-start(f32[2,3072]{1,0:T(2,128)} %param.9) | copy-start | bytes 73732
  92.5 111.3 %all-to-all-start = ((bf16[2,18432,128]{2,0,1:T(2,128)(2,1)}), bf16[2,18432,128]{2,0,1:T(2,128)(2,1)}, u32[]{:S(2)}, u32[]{:S(2)}) async-start(bf16[2,18432,128]{2,0,1:T(2,128)(2,1)} %all-gather.2.cloned.1.call-done), calls=%async_computation | async-start | bytes 18874368 | tf_op jit(solution)/shard_map/all_to_all | solution.py:68
  97.6 647.1 %all-reduce.3.cloned.1.call-start = ((), (), s32[]{:S(2)}) async-start(), calls=%async_computation.2 | async-start | bytes 4718592 | tf_op jit(solution)/shard_map/psum | solution.py:88
  282.6 18.3 %copy-start.2 = (f32[2304,192]{1,0:T(8,128)S(1)}, f32[2304,192]{1,0:T(8,128)}, u32[]{:S(2)}) copy-start(f32[2304,192]{1,0:T(8,128)} %get-tuple-element.199) | copy-start | bytes 5308420 | tf_op jit(solution)/shard_map/while
  325.0 18.3 %copy-start.2 = (f32[2304,192]{1,0:T(8,128)S(1)}, f32[2304,192]{1,0:T(8,128)}, u32[]{:S(2)}) copy-start(f32[2304,192]{1,0:T(8,128)} %get-tuple-element.199) | copy-start | bytes 5308420 | tf_op jit(solution)/shard_map/while
  367.3 18.3 %copy-start.2 = (f32[2304,192]{1,0:T(8,128)S(1)}, f32[2304,192]{1,0:T(8,128)}, u32[]{:S(2)}) copy-start(f32[2304,192]{1,0:T(8,128)} %get-tuple-element.199) | copy-start | bytes 5308420 | tf_op jit(solution)/shard_map/while
  409.7 18.3 %copy-start.2 = (f32[2304,192]{1,0:T(8,128)S(1)}, f32[2304,192]{1,0:T(8,128)}, u32[]{:S(2)}) copy-start(f32[2304,192]{1,0:T(8,128)} %get-tuple-element.199) | copy-start | bytes 5308420 | tf_op jit(solution)/shard_map/while
  452.1 18.3 %copy-start.2 = (f32[2304,192]{1,0:T(8,128)S(1)}, f32[2304,192]{1,0:T(8,128)}, u32[]{:S(2)}) copy-start(f32[2304,192]{1,0:T(8,128)} %get-tuple-element.199) | copy-start | bytes 5308420 | tf_op jit(solution)/shard_map/while
  494.5 18.3 %copy-start.2 = (f32[2304,192]{1,0:T(8,128)S(1)}, f32[2304,192]{1,0:T(8,128)}, u32[]{:S(2)}) copy-start(f32[2304,192]{1,0:T(8,128)} %get-tuple-element.199) | copy-start | bytes 5308420 | tf_op jit(solution)/shard_map/while
  536.8 18.3 %copy-start.2 = (f32[2304,192]{1,0:T(8,128)S(1)}, f32[2304,192]{1,0:T(8,128)}, u32[]{:S(2)}) copy-start(f32[2304,192]{1,0:T(8,128)} %get-tuple-element.199) | copy-start | bytes 5308420 | tf_op jit(solution)/shard_map/while
  579.2 18.3 %copy-start.2 = (f32[2304,192]{1,0:T(8,128)S(1)}, f32[2304,192]{1,0:T(8,128)}, u32[]{:S(2)}) copy-start(f32[2304,192]{1,0:T(8,128)} %get-tuple-element.199) | copy-start | bytes 5308420 | tf_op jit(solution)/shard_map/while
  627.7 0.7 copy-start.5
  627.7 0.9 copy-start.3
  627.8 255.3 %all-reduce.5.cloned.1.call-start = ((), (), s32[]{:S(2)}) async-start(), calls=%async_computation.3 | async-start | bytes 393216 | tf_op jit(solution)/shard_map/psum | solution.py:90
  744.7 2.4 copy-start.1
Sparse Core Ops, SparseCore 0:
  12.7 79.7 all-gather.1
  627.9 116.7 all-reduce.2
  749.6 133.4 all-reduce.4
where the time goes:
time: 901 us; the launch traced here: 891 us
  waiting for transfers between devices  433 us (48%)
  matrix products  282 us (31%)
  local copies, waits for them, and re-layouts  127 us (14%)
  loops' own time  25.6 us (3%)
  between operations  13.4 us (1%)
    dot_general x8, matrix products, orbital_block(): jnp.dot(sine_part, right_sin, precision=lax.Precision.HIGHEST, preferred_...  146 us
    psum x1, waiting for transfers between devices, local(): return lax.psum(gradient, 'walk')  134 us
    dot_general x8, matrix products, orbital_block(): jnp.dot(cosine, right_cos, precision=lax.Precision.HIGHEST, preferred_ele...  131 us
    psum x1, waiting for transfers between devices, local(): orbitals = lax.psum(partial_value, 'band')  114 us
    all_to_all x1, waiting for transfers between devices, local(): lax.all_to_all(gathered, 'band', split_axis=1, concat_axis=2, tiled=True)  105 us
    all_gather x1, waiting for transfers between devices, local(): gathered = lax.all_gather(coefficients, 'walk', axis=1, tiled=True)  79.9 us
    dynamic_update_slice x16, local copies, waits for them, and re-layouts, local(): lax.map(lambda coords: orbital_block(coords[0], coords[1], lat_x, lat_y,...  60.7 us
    all_to_all x3, local copies, waits for them, and re-layouts, local(): lax.all_to_all(gathered, 'band', split_axis=1, concat_axis=2, tiled=True)  41.4 us
  transfers between devices with their start and end apart: 4, of which 4 were waited for; matrix products, arithmetic and copies ran while one was open for 0% of the time, Pallas kernels for 0%

commit v1 on v0

--- a/solution.py
+++ b/solution.py
@@ -64,7 +64,9 @@
     band_index = lax.axis_index("band")
     occ_flat = occupied.reshape(-1)
     wave_count = lattice.shape[1]
-    gathered = lax.all_gather(coefficients, "walk", axis=1, tiled=True)
+    gathered = jnp.concatenate(
+        lax.all_to_all(jnp.stack([coefficients] * lax.axis_size("walk")), "walk", 0, 0), axis=1
+    )
     band_panel = lax.all_to_all(gathered, "band", split_axis=1, concat_axis=2, tiled=True)
     picked = jnp.take(band_panel, occ_flat, axis=2)
     local_lattice = lax.dynamic_slice_in_dim(

time: 901 us -> 961 us (1.067)
  blocking collectives: 0 us -> 116 us
  waiting for transfers between devices: 433 us -> 353 us
  local copies, waits for them, and re-layouts: 127 us -> 151 us
    all_to_all x0 -> x1, blocking collectives: none -> 116 us  [local(): lax.all_to_all(jnp.stack([coefficients] * lax.axis_size('walk')), 'walk',...]
    all_gather x1 -> x0, waiting for transfers between devices: 79.9 us -> none  [local(): gathered = lax.all_gather(coefficients, 'walk', axis=1, tiled=True)]
    reshape x0 -> x1, local copies, waits for them, and re-layouts: none -> 18.2 us  [local(): jnp.concatenate(lax.all_to_all(jnp.stack([coefficients] * lax.axis_size('...]
  transfers between devices with their start and end apart: 4 -> 3, of which waited for: 4 -> 3; matrix products, arithmetic and copies ran while one was open for 0% -> 0% of each run, Pallas kernels for 0% -> 0%
where the time goes in v1:
time: 961 us; the launch traced here: 951 us
  waiting for transfers between devices  353 us (37%)
  matrix products  282 us (29%)
  local copies, waits for them, and re-layouts  151 us (16%)
  blocking collectives  116 us (12%)
  loops' own time  25.6 us (3%)
  between operations  13.7 us (1%)
    dot_general x8, matrix products, orbital_block(): jnp.dot(sine_part, right_sin, precision=lax.Precision.HIGHEST, preferred_...  147 us
    psum x1, waiting for transfers between devices, local(): return lax.psum(gradient, 'walk')  134 us
    dot_general x8, matrix products, orbital_block(): jnp.dot(cosine, right_cos, precision=lax.Precision.HIGHEST, preferred_ele...  131 us
    all_to_all x1, blocking collectives, local(): lax.all_to_all(jnp.stack([coefficients] * lax.axis_size('walk')), 'walk',...  116 us
    psum x1, waiting for transfers between devices, local(): orbitals = lax.psum(partial_value, 'band')  115 us
    all_to_all x1, waiting for transfers between devices, local(): lax.all_to_all(gathered, 'band', split_axis=1, concat_axis=2, tiled=True)  104 us
    dynamic_update_slice x16, local copies, waits for them, and re-layouts, local(): lax.map(lambda coords: orbital_block(coords[0], coords[1], lat_x, lat_y,...  60.7 us
    all_to_all x3, local copies, waits for them, and re-layouts, local(): lax.all_to_all(gathered, 'band', split_axis=1, concat_axis=2, tiled=True)  41.1 us
  transfers between devices with their start and end apart: 3, of which 3 were waited for; matrix products, arithmetic and copies ran while one was open for 0% of the time, Pallas kernels for 0%

profile of v1, /device:TPU:0, one launch (start us, length us, event | category | flops | bytes accessed | tf_op | source)
XLA Modules:
  0.0 951.2 jit_solution(10290788740964632432)
XLA Ops:
  6.5 3.3 stack.2
  9.8 115.9 %all_to_all.23 = bf16[16,2,1152,128]{3,2,1,0:T(8,128)(2,1)} all-to-all(bf16[16,2,1152,128]{3,2,1,0:T(8,128)(2,1)S(1)} %stack.2), channel_id=1, replica_groups=mesh['walk'=16,'band'=8] {'walk'}, dimensions={0} | all-to-all | bytes 18874368 | tf_op jit(solution)/shard_map/all_to_all | solution.py:68
  125.7 8.3 copy.31
  134.1 18.2 %copy.32 = bf16[2,18432,128]{2,0,1:T(2,128)(2,1)} copy(bf16[2,18432,128]{2,1,0:T(8,128)(2,1)} %bitcast.36) | data formatting | bytes 18874368 | tf_op jit(solution)/shard_map/reshape | solution.py:67
  152.3 5.2 all-to-all-start.1
  157.8 0.9 fusion.32
  158.7 104.0 %all-to-all-done.1 = bf16[2,18432,128]{2,0,1:T(2,128)(2,1)} async-done(((bf16[2,18432,128]{2,0,1:T(2,128)(2,1)}), bf16[2,18432,128]{2,0,1:T(2,128)(2,1)}, u32[]{:S(2)}, u32[]{:S(2)}) %all-to-all-start.1) | async-done | bytes 9437216 | tf_op jit(solution)/shard_map/all_to_all | solution.py:70
  262.8 10.1 %copy.33 = bf16[2,18432,128]{2,1,0:T(8,128)(2,1)} copy(bf16[2,18432,128]{2,0,1:T(2,128)(2,1)} %all-to-all-done.1) | data formatting | bytes 18874368 | tf_op jit(solution)/shard_map/all_to_all | solution.py:70
  272.9 12.6 %copy.34 = bf16[2,2304,8,128]{1,3,2,0:T(8,128)(2,1)} copy(bf16[2,2304,8,128]{3,1,2,0:T(8,128)(2,1)} %bitcast.37) | data formatting | bytes 18874368 | tf_op jit(solution)/shard_map/all_to_all | solution.py:70
  285.5 18.4 %copy.35 = bf16[2,2304,1024]{1,0,2:T(2,128)(2,1)} copy(bf16[2,2304,1024]{1,2,0:T(8,128)(2,1)} %bitcast.38) | data formatting | bytes 18874368 | tf_op jit(solution)/shard_map/all_to_all | solution.py:70
  303.8 6.1 gather_fusion
  309.9 0.8 fusion.31
  310.8 1.2 fusion.37
  312.2 1.5 maximum_convert_fusion.1
  313.6 3.0 copy.36
  316.6 1.9 copy.37
  318.5 364.3 %while.10 = (s32[]{:T(128)}, f32[8,384,192]{1,0,2:T(8,128)}, f32[8,384]{1,0:T(8,128)S(1)}, f32[2304]{0:T(1024)S(1)}, f32[8,384]{1,0:T(8,128)S(1)}, /*index=5*/f3...) while((s32[]{:T(128)}, f32[8,384,192]{1,0,2:T(8,128)}, ...), condition=%wide.region_1.2_spmd, body=%wide.region_0.1_spmd.sunk | while | flops 4084015104 | bytes 12730505 | solution.py:84
  341.2 18.3 %fusion.54 = f32[384,192]{0,1:T(8,128)S(1)} fusion(f32[2304,192]{1,0:T(8,128)} %get-tuple-element.200, f32[2304]{0:T(1024)S(1)} %get-tuple-element.198, f32[384]{0:T(512)S(1)} %get-tuple-element.171, f32[2304]{0:T(1024)S(1)} %get-tuple-element.196, f32[384]{0:T(512)S(1)} %get-tuple-element.172), kind=kOutput, calls=%fused_computation.1.clone.1 | convolution fusion | flops 2041970688 | bytes 2085888 | tf_op jit(solution)/shard_map/while/body/eval_jaxpr/dot_general | solution.py:17
  359.5 16.4 %fusion.55 = f32[1,384,192]{1,2,0:T(8,128)S(1)} fusion(f32[384,192]{0,1:T(8,128)S(1)} %fusion.54, f32[2304,192]{1,0:T(8,128)S(1)} %copy-done.2, f32[2304]{0:T(1024)S(1)} %get-tuple-element.198, f32[384]{0:T(512)S(1)} %get-tuple-element.171, f32[2304]{0:T(1024)S(1)} %get-tuple-element.196, f32[384]{0:T(512)S(1)} %get-tuple-element.172), kind=kOutput, calls=%fused_computation.17.clone.1 | convolution fusion | flops 2042044416 | bytes 2380800 | tf_op jit(solution)/shard_map/while/body/eval_jaxpr/dot_general | solution.py:14
  376.2 7.3 dynamic_update_slice.5
  383.5 18.3 %fusion.54 = f32[384,192]{0,1:T(8,128)S(1)} fusion(f32[2304,192]{1,0:T(8,128)} %get-tuple-element.200, f32[2304]{0:T(1024)S(1)} %get-tuple-element.198, f32[384]{0:T(512)S(1)} %get-tuple-element.171, f32[2304]{0:T(1024)S(1)} %get-tuple-element.196, f32[384]{0:T(512)S(1)} %get-tuple-element.172), kind=kOutput, calls=%fused_computation.1.clone.1 | convolution fusion | flops 2041970688 | bytes 2085888 | tf_op jit(solution)/shard_map/while/body/eval_jaxpr/dot_general | solution.py:17
  401.9 16.4 %fusion.55 = f32[1,384,192]{1,2,0:T(8,128)S(1)} fusion(f32[384,192]{0,1:T(8,128)S(1)} %fusion.54, f32[2304,192]{1,0:T(8,128)S(1)} %copy-done.2, f32[2304]{0:T(1024)S(1)} %get-tuple-element.198, f32[384]{0:T(512)S(1)} %get-tuple-element.171, f32[2304]{0:T(1024)S(1)} %get-tuple-element.196, f32[384]{0:T(512)S(1)} %get-tuple-element.172), kind=kOutput, calls=%fused_computation.17.clone.1 | convolution fusion | flops 2042044416 | bytes 2380800 | tf_op jit(solution)/shard_map/while/body/eval_jaxpr/dot_general | solution.py:14
  418.6 7.3 dynamic_update_slice.5
  425.9 18.3 %fusion.54 = f32[384,192]{0,1:T(8,128)S(1)} fusion(f32[2304,192]{1,0:T(8,128)} %get-tuple-element.200, f32[2304]{0:T(1024)S(1)} %get-tuple-element.198, f32[384]{0:T(512)S(1)} %get-tuple-element.171, f32[2304]{0:T(1024)S(1)} %get-tuple-element.196, f32[384]{0:T(512)S(1)} %get-tuple-element.172), kind=kOutput, calls=%fused_computation.1.clone.1 | convolution fusion | flops 2041970688 | bytes 2085888 | tf_op jit(solution)/shard_map/while/body/eval_jaxpr/dot_general | solution.py:17
  444.3 16.4 %fusion.55 = f32[1,384,192]{1,2,0:T(8,128)S(1)} fusion(f32[384,192]{0,1:T(8,128)S(1)} %fusion.54, f32[2304,192]{1,0:T(8,128)S(1)} %copy-done.2, f32[2304]{0:T(1024)S(1)} %get-tuple-element.198, f32[384]{0:T(512)S(1)} %get-tuple-element.171, f32[2304]{0:T(1024)S(1)} %get-tuple-element.196, f32[384]{0:T(512)S(1)} %get-tuple-element.172), kind=kOutput, calls=%fused_computation.17.clone.1 | convolution fusion | flops 2042044416 | bytes 2380800 | tf_op jit(solution)/shard_map/while/body/eval_jaxpr/dot_general | solution.py:14
  461.0 7.3 dynamic_update_slice.5
  468.3 18.3 %fusion.54 = f32[384,192]{0,1:T(8,128)S(1)} fusion(f32[2304,192]{1,0:T(8,128)} %get-tuple-element.200, f32[2304]{0:T(1024)S(1)} %get-tuple-element.198, f32[384]{0:T(512)S(1)} %get-tuple-element.171, f32[2304]{0:T(1024)S(1)} %get-tuple-element.196, f32[384]{0:T(512)S(1)} %get-tuple-element.172), kind=kOutput, calls=%fused_computation.1.clone.1 | convolution fusion | flops 2041970688 | bytes 2085888 | tf_op jit(solution)/shard_map/while/body/eval_jaxpr/dot_general | solution.py:17
  486.6 16.4 %fusion.55 = f32[1,384,192]{1,2,0:T(8,128)S(1)} fusion(f32[384,192]{0,1:T(8,128)S(1)} %fusion.54, f32[2304,192]{1,0:T(8,128)S(1)} %copy-done.2, f32[2304]{0:T(1024)S(1)} %get-tuple-element.198, f32[384]{0:T(512)S(1)} %get-tuple-element.171, f32[2304]{0:T(1024)S(1)} %get-tuple-element.196, f32[384]{0:T(512)S(1)} %get-tuple-element.172), kind=kOutput, calls=%fused_computation.17.clone.1 | convolution fusion | flops 2042044416 | bytes 2380800 | tf_op jit(solution)/shard_map/while/body/eval_jaxpr/dot_general | solution.py:14
  503.4 7.3 dynamic_update_slice.5
  510.7 18.3 %fusion.54 = f32[384,192]{0,1:T(8,128)S(1)} fusion(f32[2304,192]{1,0:T(8,128)} %get-tuple-element.200, f32[2304]{0:T(1024)S(1)} %get-tuple-element.198, f32[384]{0:T(512)S(1)} %get-tuple-element.171, f32[2304]{0:T(1024)S(1)} %get-tuple-element.196, f32[384]{0:T(512)S(1)} %get-tuple-element.172), kind=kOutput, calls=%fused_computation.1.clone.1 | convolution fusion | flops 2041970688 | bytes 2085888 | tf_op jit(solution)/shard_map/while/body/eval_jaxpr/dot_general | solution.py:17
  529.0 16.4 %fusion.55 = f32[1,384,192]{1,2,0:T(8,128)S(1)} fusion(f32[384,192]{0,1:T(8,128)S(1)} %fusion.54, f32[2304,192]{1,0:T(8,128)S(1)} %copy-done.2, f32[2304]{0:T(1024)S(1)} %get-tuple-element.198, f32[384]{0:T(512)S(1)} %get-tuple-element.171, f32[2304]{0:T(1024)S(1)} %get-tuple-element.196, f32[384]{0:T(512)S(1)} %get-tuple-element.172), kind=kOutput, calls=%fused_computation.17.clone.1 | convolution fusion | flops 2042044416 | bytes 2380800 | tf_op jit(solution)/shard_map/while/body/eval_jaxpr/dot_general | solution.py:14
  545.7 7.3 dynamic_update_slice.5
  553.0 18.3 %fusion.54 = f32[384,192]{0,1:T(8,128)S(1)} fusion(f32[2304,192]{1,0:T(8,128)} %get-tuple-element.200, f32[2304]{0:T(1024)S(1)} %get-tuple-element.198, f32[384]{0:T(512)S(1)} %get-tuple-element.171, f32[2304]{0:T(1024)S(1)} %get-tuple-element.196, f32[384]{0:T(512)S(1)} %get-tuple-element.172), kind=kOutput, calls=%fused_computation.1.clone.1 | convolution fusion | flops 2041970688 | bytes 2085888 | tf_op jit(solution)/shard_map/while/body/eval_jaxpr/dot_general | solution.py:17
  571.4 16.4 %fusion.55 = f32[1,384,192]{1,2,0:T(8,128)S(1)} fusion(f32[384,192]{0,1:T(8,128)S(1)} %fusion.54, f32[2304,192]{1,0:T(8,128)S(1)} %copy-done.2, f32[2304]{0:T(1024)S(1)} %get-tuple-element.198, f32[384]{0:T(512)S(1)} %get-tuple-element.171, f32[2304]{0:T(1024)S(1)} %get-tuple-element.196, f32[384]{0:T(512)S(1)} %get-tuple-element.172), kind=kOutput, calls=%fused_computation.17.clone.1 | convolution fusion | flops 2042044416 | bytes 2380800 | tf_op jit(solution)/shard_map/while/body/eval_jaxpr/dot_general | solution.py:14
  588.1 7.3 dynamic_update_slice.5
  595.4 18.3 %fusion.54 = f32[384,192]{0,1:T(8,128)S(1)} fusion(f32[2304,192]{1,0:T(8,128)} %get-tuple-element.200, f32[2304]{0:T(1024)S(1)} %get-tuple-element.198, f32[384]{0:T(512)S(1)} %get-tuple-element.171, f32[2304]{0:T(1024)S(1)} %get-tuple-element.196, f32[384]{0:T(512)S(1)} %get-tuple-element.172), kind=kOutput, calls=%fused_computation.1.clone.1 | convolution fusion | flops 2041970688 | bytes 2085888 | tf_op jit(solution)/shard_map/while/body/eval_jaxpr/dot_general | solution.py:17
  613.8 16.4 %fusion.55 = f32[1,384,192]{1,2,0:T(8,128)S(1)} fusion(f32[384,192]{0,1:T(8,128)S(1)} %fusion.54, f32[2304,192]{1,0:T(8,128)S(1)} %copy-done.2, f32[2304]{0:T(1024)S(1)} %get-tuple-element.198, f32[384]{0:T(512)S(1)} %get-tuple-element.171, f32[2304]{0:T(1024)S(1)} %get-tuple-element.196, f32[384]{0:T(512)S(1)} %get-tuple-element.172), kind=kOutput, calls=%fused_computation.17.clone.1 | convolution fusion | flops 2042044416 | bytes 2380800 | tf_op jit(solution)/shard_map/while/body/eval_jaxpr/dot_general | solution.py:14
  630.5 7.3 dynamic_update_slice.5
  637.8 18.3 %fusion.54 = f32[384,192]{0,1:T(8,128)S(1)} fusion(f32[2304,192]{1,0:T(8,128)} %get-tuple-element.200, f32[2304]{0:T(1024)S(1)} %get-tuple-element.198, f32[384]{0:T(512)S(1)} %get-tuple-element.171, f32[2304]{0:T(1024)S(1)} %get-tuple-element.196, f32[384]{0:T(512)S(1)} %get-tuple-element.172), kind=kOutput, calls=%fused_computation.1.clone.1 | convolution fusion | flops 2041970688 | bytes 2085888 | tf_op jit(solution)/shard_map/while/body/eval_jaxpr/dot_general | solution.py:17
  656.1 16.4 %fusion.55 = f32[1,384,192]{1,2,0:T(8,128)S(1)} fusion(f32[384,192]{0,1:T(8,128)S(1)} %fusion.54, f32[2304,192]{1,0:T(8,128)S(1)} %copy-done.2, f32[2304]{0:T(1024)S(1)} %get-tuple-element.198, f32[384]{0:T(512)S(1)} %get-tuple-element.171, f32[2304]{0:T(1024)S(1)} %get-tuple-element.196, f32[384]{0:T(512)S(1)} %get-tuple-element.172), kind=kOutput, calls=%fused_computation.17.clone.1 | convolution fusion | flops 2042044416 | bytes 2380800 | tf_op jit(solution)/shard_map/while/body/eval_jaxpr/dot_general | solution.py:14
  672.9 7.3 dynamic_update_slice.5
  682.8 3.5 copy.43
  687.2 2.1 fusion.38
  689.3 114.8 %all-reduce.3.cloned.1.call-done = f32[3072,192]{0,1:T(8,128)} async-done(((f32[3072,192]{0,1:T(8,128)}), f32[3072,192]{0,1:T(8,128)}) %all-reduce.3.cloned.1.call-update) | async-done | bytes 2359312 | tf_op jit(solution)/shard_map/psum | solution.py:90
  804.1 1.9 slice_select_fusion.2
  806.9 1.9 fusion.28
  808.8 133.8 %all-reduce.5.cloned.1.call-done = f32[256,192]{0,1:T(8,128)} async-done(((f32[256,192]{0,1:T(8,128)}), f32[256,192]{0,1:T(8,128)}) %all-reduce.5.cloned.1.call-update) | async-done | bytes 196624 | tf_op jit(solution)/shard_map/psum | solution.py:92
  942.6 1.6 copy.59
  (61 shorter events, 4.9 us)
Async XLA Ops:
  6.5 680.5 %copy-start = (bf16[3072,256]{1,0:T(8,128)(2,1)S(1)}, bf16[3072,256]{1,0:T(8,128)(2,1)}, u32[]{:S(2)}) copy-start(bf16[3072,256]{1,0:T(8,128)(2,1)} %param.14) | copy-start | bytes 4718596
  152.3 5.3 copy-start.6
  152.3 5.4 copy-start.4
  152.3 110.5 %all-to-all-start.1 = ((bf16[2,18432,128]{2,0,1:T(2,128)(2,1)}), bf16[2,18432,128]{2,0,1:T(2,128)(2,1)}, u32[]{:S(2)}, u32[]{:S(2)}) async-start(bf16[2,18432,128]{2,0,1:T(2,128)(2,1)} %copy.32), calls=%async_computation.1 | async-start | bytes 18874368 | tf_op jit(solution)/shard_map/all_to_all | solution.py:70
  157.5 646.6 %all-reduce.3.cloned.1.call-start = ((), (), s32[]{:S(2)}) async-start(), calls=%async_computation.2 | async-start | bytes 4718592 | tf_op jit(solution)/shard_map/psum | solution.py:90
  341.2 18.3 %copy-start.2 = (f32[2304,192]{1,0:T(8,128)S(1)}, f32[2304,192]{1,0:T(8,128)}, u32[]{:S(2)}) copy-start(f32[2304,192]{1,0:T(8,128)} %get-tuple-element.199) | copy-start | bytes 5308420 | tf_op jit(solution)/shard_map/while
  383.5 18.3 %copy-start.2 = (f32[2304,192]{1,0:T(8,128)S(1)}, f32[2304,192]{1,0:T(8,128)}, u32[]{:S(2)}) copy-start(f32[2304,192]{1,0:T(8,128)} %get-tuple-element.199) | copy-start | bytes 5308420 | tf_op jit(solution)/shard_map/while
  425.9 18.3 %copy-start.2 = (f32[2304,192]{1,0:T(8,128)S(1)}, f32[2304,192]{1,0:T(8,128)}, u32[]{:S(2)}) copy-start(f32[2304,192]{1,0:T(8,128)} %get-tuple-element.199) | copy-start | bytes 5308420 | tf_op jit(solution)/shard_map/while
  468.3 18.3 %copy-start.2 = (f32[2304,192]{1,0:T(8,128)S(1)}, f32[2304,192]{1,0:T(8,128)}, u32[]{:S(2)}) copy-start(f32[2304,192]{1,0:T(8,128)} %get-tuple-element.199) | copy-start | bytes 5308420 | tf_op jit(solution)/shard_map/while
  510.7 18.3 %copy-start.2 = (f32[2304,192]{1,0:T(8,128)S(1)}, f32[2304,192]{1,0:T(8,128)}, u32[]{:S(2)}) copy-start(f32[2304,192]{1,0:T(8,128)} %get-tuple-element.199) | copy-start | bytes 5308420 | tf_op jit(solution)/shard_map/while
  553.0 18.3 %copy-start.2 = (f32[2304,192]{1,0:T(8,128)S(1)}, f32[2304,192]{1,0:T(8,128)}, u32[]{:S(2)}) copy-start(f32[2304,192]{1,0:T(8,128)} %get-tuple-element.199) | copy-start | bytes 5308420 | tf_op jit(solution)/shard_map/while
  595.4 18.3 %copy-start.2 = (f32[2304,192]{1,0:T(8,128)S(1)}, f32[2304,192]{1,0:T(8,128)}, u32[]{:S(2)}) copy-start(f32[2304,192]{1,0:T(8,128)} %get-tuple-element.199) | copy-start | bytes 5308420 | tf_op jit(solution)/shard_map/while
  637.8 18.3 %copy-start.2 = (f32[2304,192]{1,0:T(8,128)S(1)}, f32[2304,192]{1,0:T(8,128)}, u32[]{:S(2)}) copy-start(f32[2304,192]{1,0:T(8,128)} %get-tuple-element.199) | copy-start | bytes 5308420 | tf_op jit(solution)/shard_map/while
  686.3 0.7 copy-start.5
  686.3 0.9 copy-start.3
  686.3 256.3 %all-reduce.5.cloned.1.call-start = ((), (), s32[]{:S(2)}) async-start(), calls=%async_computation.3 | async-start | bytes 393216 | tf_op jit(solution)/shard_map/psum | solution.py:92
  804.1 2.4 copy-start.1
Sparse Core Ops, SparseCore 0:
  686.4 117.6 all-reduce.2
  808.9 133.5 all-reduce.4
